TPU v7x, 32 devices: a whole 2x2x4 slice. The times are simulated.
32 devices in a mesh: groups: 2 (over y), ctx: 4 (over z), fsdp: 2 (over x), dp: 2 (over core).
Axes of the slice: x: 2, y: 2, z: 4, core: 2. Of those that a mesh axis runs over, the one named last changes fastest.
Arguments:
- query_in: bfloat16 [8, 512, 1024], P(('groups', 'fsdp', 'dp'), 'ctx'), parts along dimension 0, may hold values from -11 to 11
- key_in: bfloat16 [8, 512, 1024], P(('groups', 'fsdp', 'dp'), 'ctx'), parts along dimension 0, may hold values from -11 to 11
- value_in: bfloat16 [8, 512, 1024], P(('groups', 'fsdp', 'dp'), 'ctx'), parts along dimension 0, may hold values from -6 to 6
- utt_lengths: int32 [8], P(('groups', 'fsdp', 'dp')), parts along dimension 0, may hold values from 128 to 512, as said below
- frames_in: bfloat16 [8, 512, 1536], P(('groups', 'fsdp', 'dp'), 'ctx'), parts along dimension 0, may hold values from -6 to 6
- out_weight: bfloat16 [1024, 1536], P(None, 'fsdp'), may hold values from -1.5 to 1.5
- conv_kernel: float32 [31, 1536], P(None, 'fsdp'), may hold values from -1 to 1
- conv_bias: float32 [1536], P('fsdp'), may hold values from -3 to 3
- ln_gain: float32 [1536], P('fsdp'), may hold values from 0.1 to 1.9
- cotangent: bfloat16 [8, 512, 1536], P(('groups', 'fsdp', 'dp'), 'ctx'), parts along dimension 0, may hold values from -6 to 6
Outputs:
- block_out: bfloat16 [8, 512, 1536], P(('groups', 'fsdp', 'dp'), 'ctx'), parts along dimension 0
- hidden_grad: bfloat16 [8, 512, 1536], P(('groups', 'fsdp', 'dp'), 'ctx'), parts along dimension 0
- grad_kernel: float32 [62, 1536], P('groups', 'fsdp'), parts along dimension 0
- grad_bias: float32 [3072], P(('groups', 'fsdp')), parts along dimension 0
- grad_gain: float32 [3072], P(('groups', 'fsdp')), parts along dimension 0
There are 2 independent parts, one for each index of `groups`. A program takes and returns all parts, laid end to end along the dimension named above; an argument that names none is the same for every part. Nothing has to cross between parts.
Inputs may be any that keep to these rules, and one draw needn't show every extreme that they name: `utt_lengths`: in every group one utterance is full, of 512 valid frames.
All inputs are finite; a program needn't handle non-finite values.
Results may differ from a plain program's by a relative error of at most 0.019.
Values may be sent and summed in bfloat16 or wider, within the bound.
No kernel may reach another device: no remote copies, remote signals or barrier semaphores. Data moves between devices by JAX's collectives and lax.ppermute only.
A program may use at most 64 MiB of HBM per device.

v0:
```python
import math
import jax
import jax.numpy as jnp
from jax import lax
from jax.sharding import PartitionSpec as P

HD = 64
TAPS = 31
NEG_FILL = -1e30


def extended(block, sides, width):
    for axis, dim in sides:
        count = lax.axis_size(axis)
        forward = [(i, i + 1) for i in range(count - 1)]
        backward = [(target, source) for source, target in forward]
        low = lax.ppermute(
            lax.slice_in_dim(block, block.shape[dim] - width, None, axis=dim), axis, forward
        )
        high = lax.ppermute(lax.slice_in_dim(block, 0, width, axis=dim), axis, backward)
        block = jnp.concatenate([low, block, high], axis=dim)
    return block


def absorb_block(state, query_heads, key_heads, value_heads, key_start, valid_len):
    run_max, run_sum, summed = state
    scores = jnp.einsum(
        "qhd,khd->qhk", query_heads, key_heads, preferred_element_type=jnp.float32
    ) * (1.0 / math.sqrt(HD))
    usable = key_start + jnp.arange(key_heads.shape[0]) < valid_len
    scores = jnp.where(usable, scores, NEG_FILL)
    new_max = jnp.maximum(run_max, jnp.max(scores, axis=-1))
    rescale = jnp.exp(run_max - new_max)
    weights = jnp.where(usable, jnp.exp(scores - new_max[..., None]), 0.0)
    run_sum = run_sum * rescale + jnp.sum(weights, axis=-1)
    summed = summed * rescale[..., None] + jnp.einsum(
        "qhk,khd->qhd",
        weights.astype(jnp.bfloat16),
        value_heads,
        preferred_element_type=jnp.float32,
    )
    return (new_max, run_sum, summed)


def normalize(block):
    as_float = block.astype(jnp.float32)
    average = jnp.mean(as_float, axis=-1, keepdims=True)
    centered = as_float - average
    variance = jnp.mean(centered * centered, axis=-1, keepdims=True)
    inv_scale = lax.rsqrt(variance + 1e-05)
    return (centered * inv_scale, inv_scale)


def convolve(conv_in, kernel_all, bias_all, out_rows):
    pre_act = bias_all + jnp.zeros((out_rows, conv_in.shape[1]), jnp.float32)
    for tap_index in range(TAPS):
        pre_act = pre_act + kernel_all[tap_index] * conv_in[tap_index : tap_index + out_rows]
    return pre_act


def live_of(positions, valid_len):
    return ((positions >= 0) & (positions < valid_len)).astype(jnp.float32)[:, None]


def shards(
    query_in,
    key_in,
    value_in,
    utt_lengths,
    frames_in,
    out_weight,
    conv_kernel,
    conv_bias,
    ln_gain,
    cotangent,
):
    row_count = query_in.shape[1]
    feat_width = query_in.shape[2]
    head_count = feat_width // HD
    valid_len = utt_lengths[0]
    ctx_count = lax.axis_size("ctx")
    row_offset = lax.axis_index("ctx") * row_count
    half_taps = TAPS // 2
    query_heads = query_in[0].reshape(row_count, head_count, HD)
    start_state = (
        jnp.full((row_count, head_count), NEG_FILL, jnp.float32),
        jnp.zeros((row_count, head_count), jnp.float32),
        jnp.zeros((row_count, head_count, HD), jnp.float32),
    )
    state = start_state
    first_row = jnp.int32(0)
    key_part = lax.all_gather(key_in, "ctx", axis=1, tiled=True)
    value_part = lax.all_gather(value_in, "ctx", axis=1, tiled=True)
    piece_rows = key_part.shape[1]
    block_len = math.gcd(piece_rows, 512)
    for block_start in range(0, piece_rows, block_len):
        key_heads = key_part[0, block_start : block_start + block_len].reshape(
            block_len, head_count, HD
        )
        value_heads = value_part[0, block_start : block_start + block_len].reshape(
            block_len, head_count, HD
        )
        state = absorb_block(
            state, query_heads, key_heads, value_heads, first_row + block_start, valid_len
        )
    run_max, run_sum, summed = state
    attended = (summed / run_sum[..., None]).reshape(row_count, feat_width).astype(jnp.bfloat16)
    projected = jnp.dot(
        attended,
        lax.all_gather(out_weight, "fsdp", axis=1, tiled=True),
        preferred_element_type=jnp.float32,
    )
    hidden = (frames_in[0].astype(jnp.float32) + projected).astype(jnp.bfloat16)
    kernel_all, bias_all, gain_all = (
        lax.all_gather(conv_kernel, "fsdp", axis=1, tiled=True),
        lax.all_gather(conv_bias, "fsdp", axis=0, tiled=True),
        lax.all_gather(ln_gain, "fsdp", axis=0, tiled=True),
    )
    grad_in = cotangent[0].astype(jnp.float32)
    live_mask = live_of(row_offset + jnp.arange(row_count), valid_len)
    widened = extended(hidden, (("ctx", 0),), half_taps)
    normed_ext, inv_ext = normalize(widened)
    conv_in = (
        live_of(row_offset - half_taps + jnp.arange(row_count + 2 * half_taps), valid_len)
        * normed_ext
        * gain_all
    )
    pre_act = convolve(conv_in, kernel_all, bias_all, row_count)
    gate_val = jax.nn.sigmoid(pre_act)
    grad_pre = grad_in * live_mask * gate_val * (1.0 + pre_act * (1.0 - gate_val))
    grad_wide = extended(grad_pre.astype(jnp.bfloat16), (("ctx", 0),), half_taps).astype(
        grad_pre.dtype
    )
    normed = normed_ext[half_taps : half_taps + row_count]
    inv_scale = inv_ext[half_taps : half_taps + row_count]
    block_out = (hidden.astype(jnp.float32) + live_mask * pre_act * gate_val).astype(jnp.bfloat16)
    grad_conv = jnp.zeros((row_count, grad_pre.shape[1]), jnp.float32)
    kernel_rows = []
    for tap_index in range(TAPS):
        back = 2 * half_taps - tap_index
        grad_conv = grad_conv + kernel_all[tap_index] * grad_wide[back : back + row_count]
        kernel_rows.append(jnp.sum(grad_pre * conv_in[tap_index : tap_index + row_count], axis=0))
    grad_conv = live_mask * grad_conv
    grad_hat = grad_conv * gain_all
    first_mean = jnp.mean(grad_hat, axis=-1, keepdims=True)
    second_mean = jnp.mean(grad_hat * normed, axis=-1, keepdims=True)
    hidden_grad = (grad_in + (grad_hat - first_mean - normed * second_mean) * inv_scale).astype(
        jnp.bfloat16
    )
    factor = 1.0 / math.sqrt(lax.axis_size("fsdp") * lax.axis_size("dp") * row_count * ctx_count)
    kernel_term = jnp.stack(kernel_rows) * factor
    bias_term = (jnp.sum(grad_pre, axis=0) * factor)[None]
    gain_term = (jnp.sum(grad_conv * normed, axis=0) * factor)[None]
    shares = (
        lax.psum_scatter(
            kernel_term.astype(jnp.bfloat16), "fsdp", scatter_dimension=1, tiled=True
        ).astype(jnp.float32),
        lax.psum_scatter(
            bias_term.astype(jnp.bfloat16), "fsdp", scatter_dimension=1, tiled=True
        ).astype(jnp.float32),
        lax.psum_scatter(
            gain_term.astype(jnp.bfloat16), "fsdp", scatter_dimension=1, tiled=True
        ).astype(jnp.float32),
    )
    totals = lax.psum((shares[0], shares[1], shares[2]), ("ctx", "dp"))
    return (block_out[None], hidden_grad[None], totals[0], totals[1][0], totals[2][0])


def solution(mesh):
    in_specs = (
        P(("groups", "fsdp", "dp"), "ctx", None),
        P(("groups", "fsdp", "dp"), "ctx", None),
        P(("groups", "fsdp", "dp"), "ctx", None),
        P(("groups", "fsdp", "dp")),
        P(("groups", "fsdp", "dp"), "ctx", None),
        P(None, "fsdp"),
        P(None, "fsdp"),
        P("fsdp"),
        P("fsdp"),
        P(("groups", "fsdp", "dp"), "ctx", None),
    )
    out_specs = (
        P(("groups", "fsdp", "dp"), "ctx", None),
        P(("groups", "fsdp", "dp"), "ctx", None),
        P("groups", "fsdp"),
        P(("groups", "fsdp")),
        P(("groups", "fsdp")),
    )
    return jax.shard_map(shards, mesh=mesh, in_specs=in_specs, out_specs=out_specs, check_vma=False)
```

profile of v0, /device:TPU:0, one launch (start us, length us, event | category | flops | bytes accessed | tf_op | source)
XLA Modules:
  0.0 231.5 jit_solution(14485959095688557060)
XLA Ops:
  7.2 0.7 all-gather.6.cloned.1.call-update
  7.9 0.7 all-gather.8.cloned.1.call-update
  8.7 0.7 all-gather.10.cloned.1.call-update
  10.1 1.1 copy.24
  11.2 6.7 %all_gather.22 = f32[31,1536]{1,0:T(8,128)S(1)} all-gather(f32[31,768]{1,0:T(8,128)} %param.16), channel_id=1, replica_groups=mesh['groups'=2,'ctx'=4,'fsdp'=2,'dp'=2] {'fsdp'}, dimensions={1}, use_global_device_ids=true | all-gather | bytes 285696 | tf_op jit(solution)/shard_map/all_gather | solution.py:115
  18.4 21.8 %all-gather.6.cloned.1.call-done = bf16[1,512,1024]{2,1,0:T(8,128)(2,1)} async-done(((bf16[1,128,1024]{2,1,0:T(8,128)(2,1)}), bf16[1,512,1024]{2,1,0:T(8,128)(2,1)}) %all-gather.6.cloned.1.call-update) | async-done | bytes 1048592 | tf_op jit(solution)/shard_map/all_gather | solution.py:92
  40.2 1.5 copy.23
  41.7 27.5 %all-gather.8.cloned.1.call-done = bf16[1,512,1024]{2,1,0:T(8,128)(2,1)} async-done(((bf16[1,128,1024]{2,1,0:T(8,128)(2,1)}), bf16[1,512,1024]{2,1,0:T(8,128)(2,1)}) %all-gather.8.cloned.1.call-update) | async-done | bytes 1048592 | tf_op jit(solution)/shard_map/all_gather | solution.py:93
  69.3 1.5 copy.25
  70.8 1.1 bitcast_reduce_fusion
  71.9 1.2 fusion.2
  73.1 1.5 fusion.20
  74.6 40.7 %all-gather.10.cloned.1.call-done = bf16[1024,1536]{1,0:T(8,128)(2,1)} async-done(((bf16[1024,768]{1,0:T(8,128)(2,1)}), bf16[1024,1536]{1,0:T(8,128)(2,1)}) %all-gather.10.cloned.1.call-update) | async-done | bytes 3145744 | tf_op jit(solution)/shard_map/all_gather | solution.py:110
  115.3 2.5 %fusion.4 = bf16[128,1536]{1,0:T(8,128)(2,1)S(1)} fusion(bf16[128,1024]{0,1:T(8,128)(2,1)S(1)} %bitcast.62, bf16[1024,1536]{1,0:T(8,128)(2,1)} %all-gather.10.cloned.1.call-done, bf16[1,128,1536]{2,1,0:T(8,128)(2,1)S(1)} %copy-done.1), kind=kOutput, calls=%fused_computation.8 | convolution fusion | flops 403243008 | bytes 4194304 | tf_op jit(solution)/shard_map/dot_general | solution.py:108
  117.8 3.4 %collective-permute-start = (bf16[15,1536]{1,0:T(8,128)(2,1)S(1)}, bf16[15,1536]{1,0:T(8,128)(2,1)S(1)}, u32[]{:S(2)}, u32[]{:S(2)}) collective-permute-start(bf16[15,1536]{1,0:T(8,128)(2,1)S(1)} %get-tuple-element.82), channel_id=1, source_target_pairs={{0,4},{4,8},{8,12},{1,5},{5,9},{9,13},{2,6},{6,10},{10,14},{3,7},{... | collective-permute-start | bytes 138248 | tf_op jit(solution)/shard_map/ppermute | solution.py:17
  121.2 1.3 collective-permute-start.1
  122.5 4.3 %all-gather.1 = f32[2,1,768]{2,1,0:T(1,128)S(1)} all-gather(f32[1,1,768]{2,1,0:T(1,128)S(1)} %reshape.114), channel_id=1, replica_groups=mesh['groups'=2,'ctx'=4,'fsdp'=2,'dp'=2] {'fsdp'}, dimensions={0}, use_global_device_ids=true | all-gather | bytes 9216 | tf_op jit(solution)/shard_map/all_gather | solution.py:117
  126.9 4.3 %all-gather = f32[2,1,768]{2,1,0:T(1,128)S(1)} all-gather(f32[1,1,768]{2,1,0:T(1,128)S(1)} %reshape.112), channel_id=1, replica_groups=mesh['groups'=2,'ctx'=4,'fsdp'=2,'dp'=2] {'fsdp'}, dimensions={0}, use_global_device_ids=true | all-gather | bytes 9216 | tf_op jit(solution)/shard_map/all_gather | solution.py:116
  131.6 0.3 fusion.23
  131.9 0.3 fusion.15
  132.3 6.3 %multiply_reduce_fusion.1 = (f32[1536]{0:T(1024)S(1)}, f32[1536]{0:T(1024)S(1)}, f32[1536]{0:T(1024)S(1)}, f32[1536]{0:T(1024)S(1)}, f32[1536]{0:T(1024)S(1)}, /...) fusion(f32[158,1536]{1,0:T(8,128)S(1)} %get-tuple-element.79, ...), kind=kLoop, calls=%fused_computation.90 | loop fusion | flops 21206016 | bytes 26653184 | tf_op jit(solution)/shard_map/reduce_sum | solution.py:142
  138.6 2.1 multiply_reduce_fusion.19
  140.8 4.5 %collective-permute-start.2 = (bf16[15,1536]{1,0:T(8,128)(2,1)S(1)}, bf16[15,1536]{1,0:T(8,128)(2,1)S(1)}, u32[]{:S(2)}, u32[]{:S(2)}) collective-permute-start(bf16[15,1536]{1,0:T(8,128)(2,1)S(1)} %get-tuple-element.80), channel_id=1, source_target_pairs={{0,4},{4,8},{8,12},{1,5},{5,9},{9,13},{2,6},{6,10},{10,14},{3,7},{... | collective-permute-start | bytes 138248 | tf_op jit(solution)/shard_map/ppermute | solution.py:17
  145.3 1.3 collective-permute-start.3
  146.6 1.0 reshape_bitcast_fusion.1
  147.9 1.7 fusion.59
  149.6 0.7 stack.100
  150.3 0.7 stack.101
  151.0 0.7 stack.102
  151.7 0.7 stack.103
  152.4 0.7 stack.104
  153.1 0.7 stack.105
  153.8 0.7 stack.106
  154.5 0.7 stack.107
  155.2 0.7 stack.108
  155.9 0.7 stack.96
  156.6 0.7 stack.97
  157.3 0.7 stack.98
  158.0 0.7 stack.99
  159.4 6.1 %multiply_reduce_fusion = (f32[1536]{0:T(1024)S(1)}, f32[128]{0:T(128)S(1)}, f32[128]{0:T(128)S(1)}, f32[128,1536]{1,0:T(8,128)S(1)}) fusion(f32[158,1536]{1,0:T(8,128)S(1)} %get-tuple-element.78, f32[1536]{0:T(1024)S(1)} %reshape.115, f32[158,1536]{1,0:T(8,128)S(1)} %maximum_convert_fusion, f32[1536]{0:T(1024)S(1)} %get-tuple-element.41, ...), kind=kLoop, calls=%fused_computation.89 | loop fusion | flops 13367552 | bytes 26156544 | tf_op jit(solution)/shard_map/reduce_sum | solution.py:153
  165.6 1.0 reshape_bitcast_fusion
  166.6 0.7 multiply_convert_fusion
  167.4 1.0 copy.29
  168.5 1.1 fusion.58
  169.5 11.5 %reduce-scatter.12.cloned.1.call-done = bf16[768,1]{1,0:T(8,128)(2,1)} async-done(((bf16[1536,1]{1,0:T(8,128)(2,1)}), bf16[768,1]{1,0:T(8,128)(2,1)}) %reduce-scatter.12.cloned.1.call-update) | async-done | bytes 1552
  181.0 1.0 copy.31
  182.1 11.6 %reduce-scatter.8.cloned.1.call-done = bf16[31,768]{1,0:T(8,128)(2,1)} async-done(((bf16[31,1536]{1,0:T(8,128)(2,1)}), bf16[31,768]{1,0:T(8,128)(2,1)}) %reduce-scatter.8.cloned.1.call-update) | async-done | bytes 47632 | tf_op jit(solution)/shard_map/reduce_scatter | solution.py:155
  193.7 31.0 %all-reduce.2 = (f32[31,768]{1,0:T(8,128)}, f32[768]{0:T(1024)}, f32[768]{0:T(1024)}) all-reduce(bf16[31,768]{1,0:T(8,128)(2,1)} %reduce-scatter.8.cloned.1.call-done, f32[768]{0:T(1024)S(1)} %get-tuple-element.91, f32[768]{0:T(1024)S(1)} %get-tuple-element.90), channel_id=1, replica_groups=mesh['groups'=2,'ctx'=4,'fsdp'=2,'dp'=2] {'ctx','dp'}, use_global_device_ids=true, to_apply=%region_38.39 | all-reduce | flops 25344 | bytes 155136 | tf_op jit(solution)/shard_map/psum | solution.py:165
  (71 shorter events, 2.1 us)
Async XLA Ops:
  7.2 33.1 %all-gather.6.cloned.1.call-start = ((), (), s32[]{:S(2)}) async-start(), calls=%async_computation.3 | async-start | bytes 1310720 | tf_op jit(solution)/shard_map/all_gather | solution.py:92
  7.9 61.4 %all-gather.8.cloned.1.call-start = ((), (), s32[]{:S(2)}) async-start(), calls=%async_computation.4 | async-start | bytes 1310720 | tf_op jit(solution)/shard_map/all_gather | solution.py:93
  8.6 106.6 %all-gather.10.cloned.1.call-start = ((), (), s32[]{:S(2)}) async-start(), calls=%async_computation.5 | async-start | bytes 4718592 | tf_op jit(solution)/shard_map/all_gather | solution.py:110
  9.4 158.0 %reduce-scatter.10.cloned.1.call-start = ((), (), s32[]{:S(2)}) async-start(), calls=%async_computation.7 | async-start | bytes 589824
  73.1 42.2 %copy-start.1 = (bf16[1,128,1536]{2,1,0:T(8,128)(2,1)S(1)}, bf16[1,128,1536]{2,1,0:T(8,128)(2,1)}, u32[]{:S(2)}) copy-start(bf16[1,128,1536]{2,1,0:T(8,128)(2,1)} %param.14) | copy-start | bytes 1179652
  74.5 48.0 %copy-start.5 = (f32[768]{0:T(1024)S(1)}, f32[768]{0:T(1024)}, u32[]{:S(2)}) copy-start(f32[768]{0:T(1024)} %param.18) | copy-start | bytes 9220
  74.5 52.4 %copy-start.6 = (f32[768]{0:T(1024)S(1)}, f32[768]{0:T(1024)}, u32[]{:S(2)}) copy-start(f32[768]{0:T(1024)} %param.17) | copy-start | bytes 9220
  74.6 57.7 %copy-start = (bf16[1,128,1536]{2,1,0:T(8,128)(2,1)S(1)}, bf16[1,128,1536]{2,1,0:T(8,128)(2,1)}, u32[]{:S(2)}) copy-start(bf16[1,128,1536]{2,1,0:T(8,128)(2,1)} %param.19) | copy-start | bytes 1179652
  117.8 13.5 %collective-permute-start = (bf16[15,1536]{1,0:T(8,128)(2,1)S(1)}, bf16[15,1536]{1,0:T(8,128)(2,1)S(1)}, u32[]{:S(2)}, u32[]{:S(2)}) collective-permute-start(bf16[15,1536]{1,0:T(8,128)(2,1)S(1)} %get-tuple-element.82), channel_id=1, source_target_pairs={{0,4},{4,8},{8,12},{1,5},{5,9},{9,13},{2,6},{6,10},{10,14},{3,7},{... | collective-permute-start | bytes 138248 | tf_op jit(solution)/shard_map/ppermute | solution.py:17
  121.2 10.1 %collective-permute-start.1 = (bf16[15,1536]{1,0:T(8,128)(2,1)S(1)}, bf16[15,1536]{1,0:T(8,128)(2,1)S(1)}, u32[]{:S(2)}, u32[]{:S(2)}) collective-permute-start(bf16[15,1536]{1,0:T(8,128)(2,1)S(1)} %get-tuple-element.83), channel_id=1, source_target_pairs={{4,0},{8,4},{12,8},{5,1},{9,5},{13,9},{6,2},{10,6},{14,10},{7,3},{... | collective-permute-start | bytes 138248 | tf_op jit(solution)/shard_map/ppermute | solution.py:20
  122.5 16.1 %copy-start.2 = (f32[128]{0:T(128)}, f32[128]{0:T(128)S(1)}, u32[]{:S(2)}) copy-start(f32[128]{0:T(128)S(1)} %and_convert_fusion.1) | copy-start | bytes 1540
  131.9 6.7 %copy-start.3 = (f32[158]{0:T(256)}, f32[158]{0:T(256)S(1)}, u32[]{:S(2)}) copy-start(f32[158]{0:T(256)S(1)} %add_rsqrt_fusion) | copy-start | bytes 1900
  140.8 18.5 %collective-permute-start.2 = (bf16[15,1536]{1,0:T(8,128)(2,1)S(1)}, bf16[15,1536]{1,0:T(8,128)(2,1)S(1)}, u32[]{:S(2)}, u32[]{:S(2)}) collective-permute-start(bf16[15,1536]{1,0:T(8,128)(2,1)S(1)} %get-tuple-element.80), channel_id=1, source_target_pairs={{0,4},{4,8},{8,12},{1,5},{5,9},{9,13},{2,6},{6,10},{10,14},{3,7},{... | collective-permute-start | bytes 138248 | tf_op jit(solution)/shard_map/ppermute | solution.py:17
  145.3 14.0 %collective-permute-start.3 = (bf16[15,1536]{1,0:T(8,128)(2,1)S(1)}, bf16[15,1536]{1,0:T(8,128)(2,1)S(1)}, u32[]{:S(2)}, u32[]{:S(2)}) collective-permute-start(bf16[15,1536]{1,0:T(8,128)(2,1)S(1)} %get-tuple-element.81), channel_id=1, source_target_pairs={{4,0},{8,4},{12,8},{5,1},{9,5},{13,9},{6,2},{10,6},{14,10},{7,3},{... | collective-permute-start | bytes 138248 | tf_op jit(solution)/shard_map/ppermute | solution.py:20
  147.7 33.4 %reduce-scatter.12.cloned.1.call-start = ((), (), s32[]{:S(2)}) async-start(), calls=%async_computation.8 | async-start | bytes 589824
  159.4 7.9 %copy-start.4 = (f32[158]{0:T(256)S(1)}, f32[158]{0:T(256)}, u32[]{:S(2)}) copy-start(f32[158]{0:T(256)} %copy-done.3) | copy-start | bytes 1900
  166.6 27.1 %reduce-scatter.8.cloned.1.call-start = ((), (), s32[]{:S(2)}) async-start(), calls=%async_computation.6 | async-start | bytes 147456 | tf_op jit(solution)/shard_map/reduce_scatter | solution.py:155
Sparse Core Ops, SparseCore 0:
  9.6 30.6 all-gather.5
  41.8 27.4 all-gather.7
  70.8 44.4 all-gather.9
  147.8 14.2 reduce-scatter.9
  166.7 14.2 reduce-scatter.11
  183.6 9.9 reduce-scatter.7
where the time goes:
time: 233 us; the launch traced here: 232 us
  waiting for transfers between devices  115 us (49%)
  blocking collectives  46.4 us (20%)
  other arithmetic  20.3 us (9%)
  local copies, waits for them, and re-layouts  18.4 us (8%)
  between operations  15.2 us (7%)
  starting transfers between devices  10.9 us (5%)
  matrix products  5.07 us (2%)
    all_gather x1, waiting for transfers between devices, shards(): lax.all_gather(out_weight, 'fsdp', axis=1, tiled=True)  40.7 us
    psum x1, blocking collectives, shards(): totals = lax.psum((shares[0], shares[1], shares[2]), ('ctx', 'dp'))  31 us
    all_gather x1, waiting for transfers between devices, shards(): value_part = lax.all_gather(value_in, 'ctx', axis=1, tiled=True)  27.5 us
    all_gather x1, waiting for transfers between devices, shards(): key_part = lax.all_gather(key_in, 'ctx', axis=1, tiled=True)  21.8 us
    unnamed x8, waiting for transfers between devices  13.6 us
    reduce_scatter x1, waiting for transfers between devices, shards(): lax.psum_scatter(kernel_term.astype(jnp.bfloat16), 'fsdp', scatter_dimens...  11.6 us
    another operation x32, local copies, waits for them, and re-layouts, shards(): kernel_term = jnp.stack(kernel_rows) * factor  9.55 us
    reduce_sum x2, other arithmetic, shards(): jnp.sum(grad_pre * conv_in[tap_index:tap_index + row_count], axis=0)  8.42 us
  transfers between devices with their start and end apart: 10, of which 5 were waited for; matrix products, arithmetic and copies ran while one was open for 14% of the time, Pallas kernels for 0%

commit v1 on v0

--- a/solution.py
+++ b/solution.py
@@ -89,8 +89,11 @@
     )
     state = start_state
     first_row = jnp.int32(0)
-    key_part = lax.all_gather(key_in, "ctx", axis=1, tiled=True)
-    value_part = lax.all_gather(value_in, "ctx", axis=1, tiled=True)
+    key_part, value_part = jnp.split(
+        lax.all_gather(jnp.concatenate([key_in, value_in], axis=0), "ctx", axis=1, tiled=True),
+        [key_in.shape[0]],
+        axis=0,
+    )
     piece_rows = key_part.shape[1]
     block_len = math.gcd(piece_rows, 512)
     for block_start in range(0, piece_rows, block_len):

time: 233 us -> 216 us (0.927)
  waiting for transfers between devices: 115 us -> 105 us
  local copies, waits for them, and re-layouts: 18.4 us -> 10.4 us
    all_gather x2 -> x1, waiting for transfers between devices: 49.4 us -> 37.1 us  [shards(): lax.all_gather(jnp.concatenate([key_in, value_in], axis=0), 'ctx', axis=1...]
    another operation x32, local copies, waits for them, and re-layouts: 9.55 us -> 0.52 us  [shards(): kernel_term = jnp.stack(kernel_rows) * factor]
    unnamed x8 -> x7, waiting for transfers between devices: 13.6 us -> 18.4 us
    all_gather x2 -> x0, local copies, waits for them, and re-layouts: 2.98 us -> none  [the longest x1 1.49 us: shards(): key_part = lax.all_gather(key_in, 'ctx', axis=1, tiled=True)]
    all_gather x1, waiting for transfers between devices: 40.7 us -> 37.8 us  [shards(): lax.all_gather(out_weight, 'fsdp', axis=1, tiled=True)]
    split x0 -> x3, local copies, waits for them, and re-layouts: none -> 2.8 us  [shards(): jnp.split(lax.all_gather(jnp.concatenate([key_in, value_in], axis=0), 'ct...]
    unnamed x23 -> x47, local copies, waits for them, and re-layouts: 5.28 us -> 5.33 us
  transfers between devices with their start and end apart: 10 -> 9, of which waited for: 5 -> 5; matrix products, arithmetic and copies ran while one was open for 14% -> 11% of each run, Pallas kernels for 0% -> 0%
where the time goes in v1:
time: 216 us
  waiting for transfers between devices  105 us (49%)
  blocking collectives  46.3 us (21%)
  other arithmetic  21.2 us (10%)
  between operations  15.2 us (7%)
  starting transfers between devices  12.1 us (6%)
  local copies, waits for them, and re-layouts  10.4 us (5%)
  matrix products  5.75 us (3%)
    all_gather x1, waiting for transfers between devices, shards(): lax.all_gather(out_weight, 'fsdp', axis=1, tiled=True)  37.8 us
    all_gather x1, waiting for transfers between devices, shards(): lax.all_gather(jnp.concatenate([key_in, value_in], axis=0), 'ctx', axis=1...  37.1 us
    psum x1, blocking collectives, shards(): totals = lax.psum((shares[0], shares[1], shares[2]), ('ctx', 'dp'))  31 us
    unnamed x7, waiting for transfers between devices  18.4 us
    reduce_scatter x1, waiting for transfers between devices, shards(): lax.psum_scatter(kernel_term.astype(jnp.bfloat16), 'fsdp', scatter_dimens...  11.6 us
    ppermute x2, starting transfers between devices, extended(): lax.ppermute(lax.slice_in_dim(block, block.shape[dim] - width, None, axis...  9.1 us
    reduce_sum x2, other arithmetic, shards(): jnp.sum(grad_pre * conv_in[tap_index:tap_index + row_count], axis=0)  7.78 us
    all_gather x1, blocking collectives, shards(): lax.all_gather(conv_kernel, 'fsdp', axis=1, tiled=True)  6.66 us
  transfers between devices with their start and end apart: 9, of which 5 were waited for; matrix products, arithmetic and copies ran while one was open for 11% of the time, Pallas kernels for 0%

profile of v1, /device:TPU:0, one launch (start us, length us, event | category | flops | bytes accessed | tf_op | source)
XLA Modules:
  0.0 215.8 jit_solution(8472566573849929541)
XLA Ops:
  7.2 0.0 all-gather.5.cloned.1.call-start
  7.2 1.9 pad_maximum_fusion
  9.1 0.0 all-gather.7.cloned.1.call-start
  9.2 0.7 all-gather.7.cloned.1.call-update
  9.9 0.0 reduce-scatter.10.cloned.1.call-start
  10.6 1.1 copy.24
  11.7 6.7 %all_gather.18 = f32[31,1536]{1,0:T(8,128)S(1)} all-gather(f32[31,768]{1,0:T(8,128)} %param.16), channel_id=1, replica_groups=mesh['groups'=2,'ctx'=4,'fsdp'=2,'dp'=2] {'fsdp'}, dimensions={1}, use_global_device_ids=true | all-gather | bytes 285696 | tf_op jit(solution)/shard_map/all_gather | solution.py:118
  18.4 0.5 iota_compare_fusion
  18.9 0.6 and_convert_fusion
  19.5 0.8 slice_reduce_fusion.29
  20.2 0.9 slice_reduce_fusion.30
  21.1 37.1 %all-gather.5.cloned.1.call-done = bf16[2,512,1024]{2,1,0:T(8,128)(2,1)} async-done(((bf16[2,128,1024]{2,1,0:T(8,128)(2,1)}), bf16[2,512,1024]{2,1,0:T(8,128)(2,1)}) %all-gather.5.cloned.1.call-update) | async-done | bytes 2097168 | tf_op jit(solution)/shard_map/all_gather | solution.py:93
  58.2 1.7 fusion.66
  60.0 0.5 copy.25
  60.5 0.5 copy.23
  61.1 1.8 bitcast_reduce_fusion
  62.9 1.1 fusion.2
  64.1 1.5 fusion.20
  65.7 37.8 %all-gather.7.cloned.1.call-done = bf16[1024,1536]{1,0:T(8,128)(2,1)} async-done(((bf16[1024,768]{1,0:T(8,128)(2,1)}), bf16[1024,1536]{1,0:T(8,128)(2,1)}) %all-gather.7.cloned.1.call-update) | async-done | bytes 3145744 | tf_op jit(solution)/shard_map/all_gather | solution.py:113
  103.5 2.5 %fusion.4 = bf16[128,1536]{1,0:T(8,128)(2,1)S(1)} fusion(bf16[128,1024]{0,1:T(8,128)(2,1)S(1)} %bitcast.62, bf16[1024,1536]{1,0:T(8,128)(2,1)} %all-gather.7.cloned.1.call-done, bf16[1,128,1536]{2,1,0:T(8,128)(2,1)S(1)} %copy-done.1), kind=kOutput, calls=%fused_computation.8 | convolution fusion | flops 403243008 | bytes 4194304 | tf_op jit(solution)/shard_map/dot_general | solution.py:111
  106.0 1.3 collective-permute-start.1
  107.3 4.5 %collective-permute-start = (bf16[15,1536]{1,0:T(8,128)(2,1)S(1)}, bf16[15,1536]{1,0:T(8,128)(2,1)S(1)}, u32[]{:S(2)}, u32[]{:S(2)}) collective-permute-start(bf16[15,1536]{1,0:T(8,128)(2,1)S(1)} %get-tuple-element.84), channel_id=1, source_target_pairs={{0,4},{4,8},{8,12},{1,5},{5,9},{9,13},{2,6},{6,10},{10,14},{3,7},{... | collective-permute-start | bytes 138248 | tf_op jit(solution)/shard_map/ppermute | solution.py:17
  111.9 4.3 %all-gather.1 = f32[2,1,768]{2,1,0:T(1,128)S(1)} all-gather(f32[1,1,768]{2,1,0:T(1,128)S(1)} %reshape.114), channel_id=1, replica_groups=mesh['groups'=2,'ctx'=4,'fsdp'=2,'dp'=2] {'fsdp'}, dimensions={0}, use_global_device_ids=true | all-gather | bytes 9216 | tf_op jit(solution)/shard_map/all_gather | solution.py:120
  116.3 4.3 %all-gather = f32[2,1,768]{2,1,0:T(1,128)S(1)} all-gather(f32[1,1,768]{2,1,0:T(1,128)S(1)} %reshape.112), channel_id=1, replica_groups=mesh['groups'=2,'ctx'=4,'fsdp'=2,'dp'=2] {'fsdp'}, dimensions={0}, use_global_device_ids=true | all-gather | bytes 9216 | tf_op jit(solution)/shard_map/all_gather | solution.py:119
  120.7 0.2 convert_reduce_fusion
  120.9 0.3 fusion.23
  121.3 0.3 fusion.15
  121.8 6.3 %multiply_reduce_fusion.1 = (f32[1536]{0:T(1024)S(1)}, f32[1536]{0:T(1024)S(1)}, f32[1536]{0:T(1024)S(1)}, f32[1536]{0:T(1024)S(1)}, f32[1536]{0:T(1024)S(1)}, /...) fusion(f32[158,1536]{1,0:T(8,128)S(1)} %get-tuple-element.81, ...), kind=kLoop, calls=%fused_computation.90 | loop fusion | flops 21206016 | bytes 26653184 | tf_op jit(solution)/shard_map/reduce_sum | solution.py:145
  128.1 1.0 fusion.59
  129.1 1.5 multiply_reduce_fusion.19
  130.6 1.3 collective-permute-start.3
  131.9 4.5 %collective-permute-start.2 = (bf16[15,1536]{1,0:T(8,128)(2,1)S(1)}, bf16[15,1536]{1,0:T(8,128)(2,1)S(1)}, u32[]{:S(2)}, u32[]{:S(2)}) collective-permute-start(bf16[15,1536]{1,0:T(8,128)(2,1)S(1)} %get-tuple-element.82), channel_id=1, source_target_pairs={{0,4},{4,8},{8,12},{1,5},{5,9},{9,13},{2,6},{6,10},{10,14},{3,7},{... | collective-permute-start | bytes 138248 | tf_op jit(solution)/shard_map/ppermute | solution.py:17
  136.5 1.0 reshape_bitcast_fusion.1
  137.9 0.2 reduce-scatter.12.cloned.1.call-start
  138.2 0.3 stack.127
  138.5 0.1 maximum_convert_fusion
  138.6 5.4 %multiply_reduce_fusion = (f32[1536]{0:T(1024)S(1)}, f32[128]{0:T(128)S(1)}, f32[128]{0:T(128)S(1)}, f32[128,1536]{1,0:T(8,128)S(1)}) fusion(f32[158,1536]{1,0:T(8,128)S(1)} %get-tuple-element.80, f32[1536]{0:T(1024)S(1)} %reshape.115, f32[158,1536]{1,0:T(8,128)S(1)} %maximum_convert_fusion, f32[1536]{0:T(1024)S(1)} %get-tuple-element.41, ...), kind=kLoop, calls=%fused_computation.89 | loop fusion | flops 13367552 | bytes 26156544 | tf_op jit(solution)/shard_map/reduce_sum | solution.py:156
  144.0 1.0 reshape_bitcast_fusion
  145.1 0.0 reduce-scatter.8.cloned.1.call-start
  145.1 0.7 multiply_convert_fusion
  145.8 0.1 slice.458
  145.9 4.4 %reduce-scatter.10.cloned.1.call-done = bf16[768,1]{1,0:T(8,128)(2,1)} async-done(((bf16[1536,1]{1,0:T(8,128)(2,1)}), bf16[768,1]{1,0:T(8,128)(2,1)}) %reduce-scatter.10.cloned.1.call-update) | async-done | bytes 1552
  150.3 1.0 copy.29
  151.3 1.1 fusion.58
  152.4 13.2 %reduce-scatter.12.cloned.1.call-done = bf16[768,1]{1,0:T(8,128)(2,1)} async-done(((bf16[1536,1]{1,0:T(8,128)(2,1)}), bf16[768,1]{1,0:T(8,128)(2,1)}) %reduce-scatter.12.cloned.1.call-update) | async-done | bytes 1552
  165.6 1.0 copy.31
  166.7 11.6 %reduce-scatter.8.cloned.1.call-done = bf16[31,768]{1,0:T(8,128)(2,1)} async-done(((bf16[31,1536]{1,0:T(8,128)(2,1)}), bf16[31,768]{1,0:T(8,128)(2,1)}) %reduce-scatter.8.cloned.1.call-update) | async-done | bytes 47632 | tf_op jit(solution)/shard_map/reduce_scatter | solution.py:158
  178.3 31.0 %all-reduce.2 = (f32[31,768]{1,0:T(8,128)}, f32[768]{0:T(1024)}, f32[768]{0:T(1024)}) all-reduce(bf16[31,768]{1,0:T(8,128)(2,1)} %reduce-scatter.8.cloned.1.call-done, f32[768]{0:T(1024)S(1)} %get-tuple-element.93, f32[768]{0:T(1024)S(1)} %get-tuple-element.92), channel_id=1, replica_groups=mesh['groups'=2,'ctx'=4,'fsdp'=2,'dp'=2] {'ctx','dp'}, use_global_device_ids=true, to_apply=%region_38.39 | all-reduce | flops 25344 | bytes 155136 | tf_op jit(solution)/shard_map/psum | solution.py:168
  (94 shorter events, 0.6 us)
Async XLA Ops:
  7.2 51.1 %all-gather.5.cloned.1.call-start = ((), (), s32[]{:S(2)}) async-start(), calls=%async_computation.3 | async-start | bytes 2621440 | tf_op jit(solution)/shard_map/all_gather | solution.py:93
  9.1 94.3 %all-gather.7.cloned.1.call-start = ((), (), s32[]{:S(2)}) async-start(), calls=%async_computation.4 | async-start | bytes 4718592 | tf_op jit(solution)/shard_map/all_gather | solution.py:113
  9.9 140.4 %reduce-scatter.10.cloned.1.call-start = ((), (), s32[]{:S(2)}) async-start(), calls=%async_computation.6 | async-start | bytes 589824
  61.1 1.8 copy-start.15
  64.0 39.4 %copy-start.1 = (bf16[1,128,1536]{2,1,0:T(8,128)(2,1)S(1)}, bf16[1,128,1536]{2,1,0:T(8,128)(2,1)}, u32[]{:S(2)}) copy-start(bf16[1,128,1536]{2,1,0:T(8,128)(2,1)} %param.14) | copy-start | bytes 1179652
  65.5 46.3 %copy-start.17 = (f32[768]{0:T(1024)S(1)}, f32[768]{0:T(1024)}, u32[]{:S(2)}) copy-start(f32[768]{0:T(1024)} %param.18) | copy-start | bytes 9220
  65.5 50.7 %copy-start.18 = (f32[768]{0:T(1024)S(1)}, f32[768]{0:T(1024)}, u32[]{:S(2)}) copy-start(f32[768]{0:T(1024)} %param.17) | copy-start | bytes 9220
  65.5 55.7 %copy-start.16 = (f32[158]{0:T(256)S(1)}, f32[158]{0:T(256)}, u32[]{:S(2)}) copy-start(f32[158]{0:T(256)} %and_convert_fusion) | copy-start | bytes 1900
  65.6 56.1 %copy-start = (bf16[1,128,1536]{2,1,0:T(8,128)(2,1)S(1)}, bf16[1,128,1536]{2,1,0:T(8,128)(2,1)}, u32[]{:S(2)}) copy-start(bf16[1,128,1536]{2,1,0:T(8,128)(2,1)} %param.19) | copy-start | bytes 1179652
  65.6 56.1 %copy-start.2 = (f32[1536]{0:T(1024)S(1)}, f32[1536]{0:T(1024)}, u32[]{:S(2)}) copy-start(f32[1536]{0:T(1024)} %get-tuple-element.58) | copy-start | bytes 18436
  65.6 56.1 %copy-start.3 = (f32[1536]{0:T(1024)S(1)}, f32[1536]{0:T(1024)}, u32[]{:S(2)}) copy-start(f32[1536]{0:T(1024)} %get-tuple-element.59) | copy-start | bytes 18436
  65.6 56.1 %copy-start.4 = (f32[1536]{0:T(1024)S(1)}, f32[1536]{0:T(1024)}, u32[]{:S(2)}) copy-start(f32[1536]{0:T(1024)} %get-tuple-element.60) | copy-start | bytes 18436
  65.6 56.1 %copy-start.5 = (f32[1536]{0:T(1024)S(1)}, f32[1536]{0:T(1024)}, u32[]{:S(2)}) copy-start(f32[1536]{0:T(1024)} %get-tuple-element.61) | copy-start | bytes 18436
  65.6 56.1 %copy-start.6 = (f32[1536]{0:T(1024)S(1)}, f32[1536]{0:T(1024)}, u32[]{:S(2)}) copy-start(f32[1536]{0:T(1024)} %get-tuple-element.62) | copy-start | bytes 18436
  65.6 56.1 %copy-start.7 = (f32[1536]{0:T(1024)S(1)}, f32[1536]{0:T(1024)}, u32[]{:S(2)}) copy-start(f32[1536]{0:T(1024)} %get-tuple-element.63) | copy-start | bytes 18436
  65.6 56.1 %copy-start.8 = (f32[1536]{0:T(1024)S(1)}, f32[1536]{0:T(1024)}, u32[]{:S(2)}) copy-start(f32[1536]{0:T(1024)} %get-tuple-element.64) | copy-start | bytes 18436
  65.6 56.1 %copy-start.9 = (f32[1536]{0:T(1024)S(1)}, f32[1536]{0:T(1024)}, u32[]{:S(2)}) copy-start(f32[1536]{0:T(1024)} %get-tuple-element.65) | copy-start | bytes 18436
  65.6 56.1 %copy-start.10 = (f32[1536]{0:T(1024)S(1)}, f32[1536]{0:T(1024)}, u32[]{:S(2)}) copy-start(f32[1536]{0:T(1024)} %get-tuple-element.66) | copy-start | bytes 18436
  65.7 56.1 %copy-start.11 = (f32[1536]{0:T(1024)S(1)}, f32[1536]{0:T(1024)}, u32[]{:S(2)}) copy-start(f32[1536]{0:T(1024)} %get-tuple-element.67) | copy-start | bytes 18436
  65.7 56.1 %copy-start.12 = (f32[1536]{0:T(1024)S(1)}, f32[1536]{0:T(1024)}, u32[]{:S(2)}) copy-start(f32[1536]{0:T(1024)} %get-tuple-element.68) | copy-start | bytes 18436
  65.7 56.1 %copy-start.13 = (f32[1536]{0:T(1024)S(1)}, f32[1536]{0:T(1024)}, u32[]{:S(2)}) copy-start(f32[1536]{0:T(1024)} %get-tuple-element.69) | copy-start | bytes 18436
  65.7 56.1 %copy-start.14 = (f32[1536]{0:T(1024)S(1)}, f32[1536]{0:T(1024)}, u32[]{:S(2)}) copy-start(f32[1536]{0:T(1024)} %get-tuple-element.70) | copy-start | bytes 18436
  106.0 14.7 %collective-permute-start.1 = (bf16[15,1536]{1,0:T(8,128)(2,1)S(1)}, bf16[15,1536]{1,0:T(8,128)(2,1)S(1)}, u32[]{:S(2)}, u32[]{:S(2)}) collective-permute-start(bf16[15,1536]{1,0:T(8,128)(2,1)S(1)} %get-tuple-element.85), channel_id=1, source_target_pairs={{4,0},{8,4},{12,8},{5,1},{9,5},{13,9},{6,2},{10,6},{14,10},{7,3},{... | collective-permute-start | bytes 138248 | tf_op jit(solution)/shard_map/ppermute | solution.py:20
  107.3 13.4 %collective-permute-start = (bf16[15,1536]{1,0:T(8,128)(2,1)S(1)}, bf16[15,1536]{1,0:T(8,128)(2,1)S(1)}, u32[]{:S(2)}, u32[]{:S(2)}) collective-permute-start(bf16[15,1536]{1,0:T(8,128)(2,1)S(1)} %get-tuple-element.84), channel_id=1, source_target_pairs={{0,4},{4,8},{8,12},{1,5},{5,9},{9,13},{2,6},{6,10},{10,14},{3,7},{... | collective-permute-start | bytes 138248 | tf_op jit(solution)/shard_map/ppermute | solution.py:17
  130.6 7.9 %collective-permute-start.3 = (bf16[15,1536]{1,0:T(8,128)(2,1)S(1)}, bf16[15,1536]{1,0:T(8,128)(2,1)S(1)}, u32[]{:S(2)}, u32[]{:S(2)}) collective-permute-start(bf16[15,1536]{1,0:T(8,128)(2,1)S(1)} %get-tuple-element.83), channel_id=1, source_target_pairs={{4,0},{8,4},{12,8},{5,1},{9,5},{13,9},{6,2},{10,6},{14,10},{7,3},{... | collective-permute-start | bytes 138248 | tf_op jit(solution)/shard_map/ppermute | solution.py:20
  131.9 6.6 %collective-permute-start.2 = (bf16[15,1536]{1,0:T(8,128)(2,1)S(1)}, bf16[15,1536]{1,0:T(8,128)(2,1)S(1)}, u32[]{:S(2)}, u32[]{:S(2)}) collective-permute-start(bf16[15,1536]{1,0:T(8,128)(2,1)S(1)} %get-tuple-element.82), channel_id=1, source_target_pairs={{0,4},{4,8},{8,12},{1,5},{5,9},{9,13},{2,6},{6,10},{10,14},{3,7},{... | collective-permute-start | bytes 138248 | tf_op jit(solution)/shard_map/ppermute | solution.py:17
  137.9 27.7 %reduce-scatter.12.cloned.1.call-start = ((), (), s32[]{:S(2)}) async-start(), calls=%async_computation.7 | async-start | bytes 589824
  145.1 33.2 %reduce-scatter.8.cloned.1.call-start = ((), (), s32[]{:S(2)}) async-start(), calls=%async_computation.5 | async-start | bytes 147456 | tf_op jit(solution)/shard_map/reduce_scatter | solution.py:158
Sparse Core Ops, SparseCore 0:
  9.6 48.6 all-gather.4
  59.8 43.6 all-gather.6
  138.1 12.1 reduce-scatter.9
  152.5 13.1 reduce-scatter.11
  168.2 9.9 reduce-scatter.7
